TPU v7x, 32 devices: a whole 2x2x4 slice. The times are simulated.
32 devices in a mesh: wide: 8 (over z, core), col: 4 (over y, x).
Axes of the slice: x: 2, y: 2, z: 4, core: 2. Of those that a mesh axis runs over, the one named last changes fastest.
Arguments:
- amplitudes: float32 [2048, 2048], P('wide', 'col'), may hold values from -6 to 6
- integrals: float32 [2048, 2048], P('wide', 'col'), may hold values from -0.125 to 0.125
Outputs:
- ladder: float32 [2048, 2048], P(('wide', 'col'))
All inputs are finite; a program needn't handle non-finite values.
Results may differ from a plain program's by a relative error of at most 0.00007.
Values sent between devices are 32-bit elements; how exact they have to be, the bound alone decides.
A program may use at most 64 MiB of HBM per device.

v0:
```python
import jax
import jax.numpy as jnp
from jax import lax
from jax.sharding import PartitionSpec as P


def contract(left_rows, panel):
    return lax.dot_general(
        left_rows,
        panel,
        (((1,), (1,)), ((), ())),
        precision=lax.Precision.HIGHEST,
        preferred_element_type=jnp.float32,
    )


def on_device(amplitudes, integrals):
    rows_local, cd_local = amplitudes.shape
    wide_count = lax.axis_size("wide")
    col_count = lax.axis_size("col")
    total_rows = rows_local * wide_count
    gathered = lax.all_gather(amplitudes, "wide", axis=0, tiled=True)
    share_rows = total_rows // (wide_count * col_count)
    blocks_view = gathered.reshape(wide_count, col_count, share_rows, cd_local)
    block_rows = wide_count * share_rows
    arranged = jnp.swapaxes(blocks_view, 0, 1).reshape(block_rows * lax.axis_size("col"), cd_local)
    summed = lax.psum_scatter(contract(arranged, integrals), "col", scatter_dimension=0, tiled=True)
    ladder = lax.all_to_all(summed, "wide", split_axis=0, concat_axis=1, tiled=True)
    return ladder


def solution(mesh):
    return jax.shard_map(
        on_device,
        mesh=mesh,
        in_specs=(P("wide", "col"), P("wide", "col")),
        out_specs=P(("wide", "col"), None),
        check_vma=False,
    )
```

profile of v0, /device:TPU:0, one launch (start us, length us, event | category | flops | bytes accessed | tf_op | source)
XLA Modules:
  0.0 128.2 jit_solution(13461749447731396794)
XLA Ops:
  6.5 0.0 copy-start
  6.5 0.0 all-gather.2.cloned.1.call-start
  6.5 0.7 all-gather.2.cloned.1.call-update
  7.3 0.0 reduce-scatter.2.cloned.1.call-start
  7.3 51.5 %all-gather.2.cloned.1.call-done = f32[2048,512]{1,0:T(8,128)} async-done(((f32[256,512]{1,0:T(8,128)}), f32[2048,512]{1,0:T(8,128)}) %all-gather.2.cloned.1.call-update) | async-done | bytes 4194320 | tf_op jit(solution)/shard_map/all_gather | solution.py:22
  58.8 2.8 %copy.5 = f32[4,8,64,512]{3,2,1,0:T(8,128)S(1)} copy(f32[4,8,64,512]{3,2,0,1:T(8,128)} %bitcast.11) | data formatting | bytes 8388608 | tf_op jit(solution)/shard_map/transpose | solution.py:26
  61.6 0.0 copy-done
  61.6 4.9 %fusion = f32[2048,256]{1,0:T(8,128)} fusion(f32[2048,512]{1,0:T(8,128)S(1)} %bitcast.10, f32[256,512]{1,0:T(8,128)S(1)} %copy-done), kind=kOutput, calls=%fused_computation | convolution fusion | flops 3221225472 | bytes 6815744 | tf_op jit(solution)/shard_map/dot_general | solution.py:8
  66.5 0.0 reduce-scatter.2.cloned.1.call-update
  66.5 34.1 %reduce-scatter.2.cloned.1.call-done = f32[512,256]{1,0:T(8,128)} async-done(((f32[2048,256]{1,0:T(8,128)}), f32[512,256]{1,0:T(8,128)}) %reduce-scatter.2.cloned.1.call-update) | async-done | bytes 524304 | tf_op jit(solution)/shard_map/reduce_scatter | solution.py:27
  100.6 20.0 %all_to_all.19 = f32[8,64,256]{2,1,0:T(8,128)S(1)} all-to-all(f32[8,64,256]{2,1,0:T(8,128)} %bitcast.13), channel_id=1, replica_groups=mesh['wide'=8,'col'=4] {'wide'}, dimensions={0} | all-to-all | bytes 1048576 | tf_op jit(solution)/shard_map/all_to_all | solution.py:28
  120.6 0.8 copy.7
Async XLA Ops:
  6.5 55.1 %copy-start = (f32[256,512]{1,0:T(8,128)S(1)}, f32[256,512]{1,0:T(8,128)}, u32[]{:S(2)}) copy-start(f32[256,512]{1,0:T(8,128)} %param.3) | copy-start | bytes 1572868
  6.5 52.3 %all-gather.2.cloned.1.call-start = ((), (), s32[]{:S(2)}) async-start(), calls=%async_computation.2 | async-start | bytes 4718592 | tf_op jit(solution)/shard_map/all_gather | solution.py:22
  7.3 93.3 %reduce-scatter.2.cloned.1.call-start = ((), (), s32[]{:S(2)}) async-start(), calls=%async_computation.3 | async-start | bytes 2621440 | tf_op jit(solution)/shard_map/reduce_scatter | solution.py:27
Sparse Core Ops, SparseCore 0:
  9.0 49.8 all-gather.1
  66.7 33.9 reduce-scatter.1
where the time goes:
time: 128 us
  waiting for transfers between devices  86.3 us (67%)
  blocking collectives  20 us (16%)
  between operations  13.4 us (10%)
  matrix products  4.89 us (4%)
  local copies, waits for them, and re-layouts  3.59 us (3%)
    all_gather x1, waiting for transfers between devices, on_device(): gathered = lax.all_gather(amplitudes, 'wide', axis=0, tiled=True)  51.5 us
    reduce_scatter x1, waiting for transfers between devices, on_device(): lax.psum_scatter(contract(arranged, integrals), 'col', scatter_dimension=...  34.1 us
    all_to_all x1, blocking collectives, on_device(): lax.all_to_all(summed, 'wide', split_axis=0, concat_axis=1, tiled=True)  20 us
    dot_general x1, matrix products, contract(): lax.dot_general(left_rows, panel, (((1,), (1,)), ((), ())), precision=lax...  4.89 us
    transpose x1, local copies, waits for them, and re-layouts, on_device(): jnp.swapaxes(blocks_view, 0, 1)  2.75 us
  transfers between devices with their start and end apart: 2, of which 2 were waited for; matrix products, arithmetic and copies ran while one was open for 0% of the time, Pallas kernels for 0%

commit v1 on v0

v1 whole, which is shorter than its diff:
```python
import jax
import jax.numpy as jnp
from jax import lax
from jax.sharding import PartitionSpec as P


def on_device(amplitudes, integrals):
    panel = lax.all_gather(integrals, "wide", axis=0, tiled=True)
    part = lax.dot_general(
        amplitudes,
        panel,
        (((1,), (1,)), ((), ())),
        precision=lax.Precision.HIGHEST,
        preferred_element_type=jnp.float32,
    )
    return lax.psum_scatter(part, "col", scatter_dimension=0, tiled=True)


def solution(mesh):
    return jax.shard_map(
        on_device,
        mesh=mesh,
        in_specs=(P("wide", "col"), P("wide", "col")),
        out_specs=P(("wide", "col"), None),
        check_vma=False,
    )
```

time: 128 us -> 107 us (0.84)
  blocking collectives: 20 us -> 0 us
  local copies, waits for them, and re-layouts: 3.59 us -> 0.01 us
  matrix products: 4.89 us -> 7.14 us
    all_to_all x1 -> x0, blocking collectives: 20 us -> none  [on_device(): lax.all_to_all(summed, 'wide', split_axis=0, concat_axis=1, tiled=True)]
    transpose x1 -> x0, local copies, waits for them, and re-layouts: 2.75 us -> none  [on_device(): jnp.swapaxes(blocks_view, 0, 1)]
    dot_general x1, matrix products: 4.89 us -> 7.14 us  [on_device(): lax.dot_general(amplitudes, panel, (((1,), (1,)), ((), ())), precision=la...]
where the time goes in v1:
time: 107 us
  waiting for transfers between devices  86.3 us (81%)
  between operations  13.4 us (13%)
  matrix products  7.14 us (7%)
    all_gather x1, waiting for transfers between devices, on_device(): panel = lax.all_gather(integrals, 'wide', axis=0, tiled=True)  51.5 us
    reduce_scatter x1, waiting for transfers between devices, on_device(): return lax.psum_scatter(part, 'col', scatter_dimension=0, tiled=True)  34.1 us
    dot_general x1, matrix products, on_device(): lax.dot_general(amplitudes, panel, (((1,), (1,)), ((), ())), precision=la...  7.14 us
  transfers between devices with their start and end apart: 2, of which 2 were waited for; matrix products, arithmetic and copies ran while one was open for 0% of the time, Pallas kernels for 0%

profile of v1, /device:TPU:0, one launch (start us, length us, event | category | flops | bytes accessed | tf_op | source)
XLA Modules:
  0.0 106.9 jit_solution(4373981538191259689)
XLA Ops:
  6.5 0.0 copy-start
  6.5 0.0 all-gather.2.cloned.1.call-start
  6.5 0.7 all-gather.2.cloned.1.call-update
  7.3 0.0 reduce-scatter.2.cloned.1.call-start
  7.3 51.5 %all-gather.2.cloned.1.call-done = f32[2048,512]{1,0:T(8,128)} async-done(((f32[256,512]{1,0:T(8,128)}), f32[2048,512]{1,0:T(8,128)}) %all-gather.2.cloned.1.call-update) | async-done | bytes 4194320 | tf_op jit(solution)/shard_map/all_gather | solution.py:8
  58.8 0.0 copy-done
  58.8 7.1 %fusion = f32[256,2048]{1,0:T(8,128)} fusion(f32[256,512]{1,0:T(8,128)S(1)} %copy-done, f32[2048,512]{1,0:T(8,128)} %all-gather.2.cloned.1.call-done), kind=kOutput, calls=%fused_computation | convolution fusion | flops 3221225472 | bytes 6815744 | tf_op jit(solution)/shard_map/dot_general | solution.py:9
  66.0 0.0 reduce-scatter.2.cloned.1.call-update
  66.0 34.1 %reduce-scatter.2.cloned.1.call-done = f32[64,2048]{1,0:T(8,128)} async-done(((f32[256,2048]{1,0:T(8,128)}), f32[64,2048]{1,0:T(8,128)}) %reduce-scatter.2.cloned.1.call-update) | async-done | bytes 524304 | tf_op jit(solution)/shard_map/reduce_scatter | solution.py:16
Async XLA Ops:
  6.5 52.3 %copy-start = (f32[256,512]{1,0:T(8,128)S(1)}, f32[256,512]{1,0:T(8,128)}, u32[]{:S(2)}) copy-start(f32[256,512]{1,0:T(8,128)} %param.2) | copy-start | bytes 1572868
  6.5 52.3 %all-gather.2.cloned.1.call-start = ((), (), s32[]{:S(2)}) async-start(), calls=%async_computation.1 | async-start | bytes 4718592 | tf_op jit(solution)/shard_map/all_gather | solution.py:8
  7.3 92.8 %reduce-scatter.2.cloned.1.call-start = ((), (), s32[]{:S(2)}) async-start(), calls=%async_computation.2 | async-start | bytes 2621440 | tf_op jit(solution)/shard_map/reduce_scatter | solution.py:16
Sparse Core Ops, SparseCore 0:
  9.0 49.8 all-gather.1
  66.1 33.9 reduce-scatter.1

commit v2 on v1

v2 whole, which is shorter than its diff:
```python
import functools

import jax
import jax.numpy as jnp
from jax import lax
from jax.experimental import pallas as pl
from jax.experimental.pallas import tpu as pltpu
from jax.sharding import PartitionSpec as P

MESH = pl.DeviceIdType.MESH
CORES = 2
PIECES = 2


def halves(x):
    high = x.astype(jnp.bfloat16)
    low = (x - high.astype(jnp.float32)).astype(jnp.bfloat16)
    return high, low


def dot(x, y):
    return lax.dot_general(x, y, (((1,), (1,)), ((), ())), preferred_element_type=jnp.float32)


def kernel(wide, cols, a_ref, b_ref, o_ref, panel, a_high, a_low, part, landed,
           send_line, send_pair, recv_panel, send_sum, recv_sum):
    w = lax.axis_index("wide")
    c = lax.axis_index("col")
    line = wide // CORES
    g = w // CORES
    core = w % CORES
    sibling = g * CORES + 1 - core
    rows = b_ref.shape[0] // PIECES
    share = o_ref.shape[0]

    barrier = pltpu.get_barrier_semaphore()

    def greet(wide_index, col_index):
        pl.semaphore_signal(barrier, inc=1, device_id={"wide": wide_index, "col": col_index}, device_id_type=MESH)

    has_left = g > 0
    has_right = g < line - 1
    pl.when(has_left)(lambda: greet(w - CORES, c))
    pl.when(has_right)(lambda: greet(w + CORES, c))
    greet(sibling, c)

    @pl.loop(1, cols)
    def _(j):
        greet(w, (c + j) % cols)

    pl.semaphore_wait(barrier, cols + has_left.astype(jnp.int32) + has_right.astype(jnp.int32))

    def push(src, slot, sem, target):
        return pltpu.make_async_remote_copy(
            src_ref=src, dst_ref=panel.at[slot], send_sem=sem, recv_sem=recv_panel.at[slot],
            device_id={"wide": target, "col": c}, device_id_type=MESH)

    def own(h):
        return b_ref.at[pl.ds(h * rows, rows)]

    def arrive(slot):
        pltpu.make_async_copy(panel.at[slot], panel.at[slot], recv_panel.at[slot]).wait()

    def contract(block, slot):
        high, low = halves(block)
        product = dot(a_high[...], high) + (dot(a_high[...], low) + dot(a_low[...], high))
        for k in range(cols):
            part[slot, k] = product[k * share:(k + 1) * share]

        @pl.loop(1, cols)
        def _(j):
            peer = (c + j) % cols
            pltpu.make_async_remote_copy(
                src_ref=part.at[slot, peer], dst_ref=landed.at[slot, cols - 1 - j],
                send_sem=send_sum.at[slot], recv_sem=recv_sum.at[slot],
                device_id={"wide": w, "col": peer}, device_id_type=MESH).start()

    for h in range(PIECES):
        slot = w * PIECES + h
        pl.when(has_right)(lambda: push(own(h), slot, send_line.at[slot], w + CORES).start())
        pl.when(has_left)(lambda: push(own(h), slot, send_line.at[wide * PIECES + h], w - CORES).start())
        push(own(h), slot, send_pair.at[slot], sibling).start()

    high, low = halves(a_ref[...])
    a_high[...] = high
    a_low[...] = low
    for h in range(PIECES):
        contract(b_ref[h * rows:(h + 1) * rows], w * PIECES + h)
    for h in range(PIECES):
        slot = sibling * PIECES + h
        arrive(slot)
        contract(panel[slot], slot)

    @pl.loop(1, line)
    def _(d):
        @pl.loop(0, PIECES)
        def _(h):
            left_slot = (w - d * CORES) * PIECES + h
            right_slot = (w + d * CORES) * PIECES + h
            pair_left = (sibling - d * CORES) * PIECES + h
            pair_right = (sibling + d * CORES) * PIECES + h

            @pl.when(g - d >= 0)
            def _():
                arrive(left_slot)
                pl.when(has_right)(lambda: push(panel.at[left_slot], left_slot, send_line.at[left_slot], w + CORES).start())
                push(panel.at[left_slot], left_slot, send_pair.at[left_slot], sibling).start()

            @pl.when(g + d < line)
            def _():
                arrive(right_slot)
                pl.when(has_left)(lambda: push(panel.at[right_slot], right_slot, send_line.at[right_slot], w - CORES).start())
                push(panel.at[right_slot], right_slot, send_pair.at[right_slot], sibling).start()

            @pl.when(g - d >= 0)
            def _():
                contract(panel[left_slot], left_slot)

            @pl.when(g + d < line)
            def _():
                contract(panel[right_slot], right_slot)

            @pl.when(g - d >= 0)
            def _():
                arrive(pair_left)
                contract(panel[pair_left], pair_left)

            @pl.when(g + d < line)
            def _():
                arrive(pair_right)
                contract(panel[pair_right], pair_right)

    @pl.loop(0, wide * PIECES)
    def _(slot):
        pltpu.make_async_copy(landed.at[slot], landed.at[slot], recv_sum.at[slot]).wait()
        total = part[slot, c]
        for k in range(cols - 1):
            total = total + landed[slot, k]
        o_ref[:, pl.ds(pl.multiple_of(slot * rows, rows), rows)] = total

    for h in range(PIECES):
        slot = w * PIECES + h
        pl.when(has_right)(lambda: push(own(h), slot, send_line.at[slot], w + CORES).wait_send())
        pl.when(has_left)(lambda: push(own(h), slot, send_line.at[wide * PIECES + h], w - CORES).wait_send())
        push(own(h), slot, send_pair.at[slot], sibling).wait_send()

    @pl.loop(1, line)
    def _(d):
        @pl.loop(0, PIECES)
        def _(h):
            left_slot = (w - d * CORES) * PIECES + h
            right_slot = (w + d * CORES) * PIECES + h

            @pl.when(g - d >= 0)
            def _():
                pl.when(has_right)(lambda: push(panel.at[left_slot], left_slot, send_line.at[left_slot], w + CORES).wait_send())
                push(panel.at[left_slot], left_slot, send_pair.at[left_slot], sibling).wait_send()

            @pl.when(g + d < line)
            def _():
                pl.when(has_left)(lambda: push(panel.at[right_slot], right_slot, send_line.at[right_slot], w - CORES).wait_send())
                push(panel.at[right_slot], right_slot, send_pair.at[right_slot], sibling).wait_send()

    @pl.loop(0, wide * PIECES)
    def _(slot):
        pltpu.make_async_copy(landed.at[slot], landed.at[slot], send_sum.at[slot]).wait()


def on_device(wide, cols, amplitudes, integrals):
    rows_a, depth = amplitudes.shape
    rows_b = integrals.shape[0]
    share = rows_a // cols
    slots = wide * PIECES
    rows = rows_b // PIECES
    vmem = pl.BlockSpec(memory_space=pltpu.VMEM)
    return pl.pallas_call(
        functools.partial(kernel, wide, cols),
        out_shape=jax.ShapeDtypeStruct((share, wide * rows_b), jnp.float32),
        in_specs=[vmem, vmem],
        out_specs=vmem,
        scratch_shapes=[
            pltpu.VMEM((slots, rows, depth), jnp.float32),
            pltpu.VMEM((rows_a, depth), jnp.bfloat16),
            pltpu.VMEM((rows_a, depth), jnp.bfloat16),
            pltpu.VMEM((slots, cols, share, rows), jnp.float32),
            pltpu.VMEM((slots, cols - 1, share, rows), jnp.float32),
            pltpu.SemaphoreType.DMA((slots + PIECES,)),
            pltpu.SemaphoreType.DMA((slots,)),
            pltpu.SemaphoreType.DMA((slots,)),
            pltpu.SemaphoreType.DMA((slots,)),
            pltpu.SemaphoreType.DMA((slots,)),
        ],
        compiler_params=pltpu.CompilerParams(
            collective_id=0, has_side_effects=True, vmem_limit_bytes=56 * 1024 * 1024),
    )(amplitudes, integrals)


def solution(mesh):
    return jax.shard_map(
        functools.partial(on_device, mesh.shape["wide"], mesh.shape["col"]),
        mesh=mesh,
        in_specs=(P("wide", "col"), P("wide", "col")),
        out_specs=P(("wide", "col"), None),
        check_vma=False,
    )
```

time: 107 us -> 49.4 us (0.46)
  waiting for transfers between devices: 86.3 us -> 0 us
  Pallas kernels: 0 us -> 47.3 us
  between operations: 13.4 us -> 0.01 us
  matrix products: 7.14 us -> 0 us
  local copies, waits for them, and re-layouts: 0.01 us -> 1.87 us
    all_gather x1 -> x0, waiting for transfers between devices: 51.5 us -> none  [on_device(): panel = lax.all_gather(integrals, 'wide', axis=0, tiled=True)]
    pallas_call x0 -> x1, Pallas kernels: none -> 47.3 us  [on_device(): pl.pallas_call(functools.partial(kernel, wide, cols), out_shape=jax.Shape...]
    reduce_scatter x1 -> x0, waiting for transfers between devices: 34.1 us -> none  [on_device(): return lax.psum_scatter(part, 'col', scatter_dimension=0, tiled=True)]
    dot_general x1 -> x0, matrix products: 7.14 us -> none  [on_device(): lax.dot_general(amplitudes, panel, (((1,), (1,)), ((), ())), precision=la...]
    unnamed x2 -> x1, local copies, waits for them, and re-layouts: 0.01 us -> 1.87 us
  transfers between devices with their start and end apart: 2 -> 0, of which waited for: 2 -> 0; matrix products, arithmetic and copies ran while one was open for 0% -> 0% of each run, Pallas kernels for 0% -> 0%
where the time goes in v2:
time: 49.4 us; the launch traced here: 49.2 us
  Pallas kernels  47.3 us (96%)
  local copies, waits for them, and re-layouts  1.87 us (4%)
    pallas_call x1, Pallas kernels, on_device(): pl.pallas_call(functools.partial(kernel, wide, cols), out_shape=jax.Shape...  47.3 us
    unnamed x1, local copies, waits for them, and re-layouts  1.87 us

profile of v2, /device:TPU:0, one launch (start us, length us, event | category | flops | bytes accessed | tf_op | source)
XLA Modules:
  0.0 49.2 jit_solution(11616142699215105814)
XLA Ops:
  0.0 47.3 %shard_map.28 = f32[64,2048]{1,0:T(8,128)} custom-call(f32[256,512]{1,0:T(8,128)} %a_ref.1, f32[256,512]{1,0:T(8,128)} %b_ref.1), custom_call_target="tpu_custom_call" | custom-call | tf_op jit(solution)/shard_map/pallas_call | solution.py:176
  47.3 1.9 %copy.4 = f32[64,2048]{1,0:T(8,128)} copy(f32[64,2048]{1,0:T(8,128)} %shard_map.28) | data formatting | bytes 1048576

commit v3 on v2

--- a/solution.py
+++ b/solution.py
@@ -23,7 +23,9 @@
 
 
 def kernel(wide, cols, a_ref, b_ref, o_ref, panel, a_high, a_low, part, landed,
-           send_line, send_pair, recv_panel, send_sum, recv_sum):
+           guest, guest_high, guest_low, outbox, inbox,
+           send_line, send_pair, recv_panel, send_sum, recv_sum,
+           send_guest, recv_guest, send_back, recv_back):
     w = lax.axis_index("wide")
     c = lax.axis_index("col")
     line = wide // CORES
@@ -32,6 +34,17 @@
     sibling = g * CORES + 1 - core
     rows = b_ref.shape[0] // PIECES
     share = o_ref.shape[0]
+    slots = wide * PIECES
+    extra = CORES * PIECES
+    far = line - 2
+    left_end, right_end = g == 0, g == line - 1
+    helps_left, helps_right = g == 1, g == far
+    is_end = left_end | right_end
+    helps = helps_left | helps_right
+    partner = jnp.where(left_end | helps_right, w + CORES, w - CORES)
+    first = jnp.where(right_end, extra, 0)
+    last = jnp.where(left_end, slots - extra, slots)
+    missing = jnp.where(left_end, slots - extra, 0)
 
     barrier = pltpu.get_barrier_semaphore()
 
@@ -61,9 +74,25 @@
     def arrive(slot):
         pltpu.make_async_copy(panel.at[slot], panel.at[slot], recv_panel.at[slot]).wait()
 
+    def lend():
+        return pltpu.make_async_remote_copy(
+            src_ref=a_ref, dst_ref=guest, send_sem=send_guest, recv_sem=recv_guest,
+            device_id={"wide": partner, "col": c}, device_id_type=MESH)
+
+    def give_back(i):
+        return pltpu.make_async_remote_copy(
+            src_ref=outbox.at[i], dst_ref=inbox.at[i], send_sem=send_back.at[i], recv_sem=recv_back.at[i],
+            device_id={"wide": partner, "col": c}, device_id_type=MESH)
+
     def contract(block, slot):
+        contract_rows(a_high, a_low, block, slot)
+
+    def contract_guest(slot):
+        contract_rows(guest_high, guest_low, panel[slot], slots + slot % extra)
+
+    def contract_rows(rows_high, rows_low, block, slot):
         high, low = halves(block)
-        product = dot(a_high[...], high) + (dot(a_high[...], low) + dot(a_low[...], high))
+        product = dot(rows_high[...], high) + (dot(rows_high[...], low) + dot(rows_low[...], high))
         for k in range(cols):
             part[slot, k] = product[k * share:(k + 1) * share]
 
@@ -91,7 +120,7 @@
         arrive(slot)
         contract(panel[slot], slot)
 
-    @pl.loop(1, line)
+    @pl.loop(1, line - 1)
     def _(d):
         @pl.loop(0, PIECES)
         def _(h):
@@ -99,18 +128,28 @@
             right_slot = (w + d * CORES) * PIECES + h
             pair_left = (sibling - d * CORES) * PIECES + h
             pair_right = (sibling + d * CORES) * PIECES + h
+            pl.when(is_end & (d == 2) & (h == 0))(lambda: lend().start())
 
             @pl.when(g - d >= 0)
             def _():
                 arrive(left_slot)
-                pl.when(has_right)(lambda: push(panel.at[left_slot], left_slot, send_line.at[left_slot], w + CORES).start())
+                pl.when(has_right & (d < far))(lambda: push(panel.at[left_slot], left_slot, send_line.at[left_slot], w + CORES).start())
                 push(panel.at[left_slot], left_slot, send_pair.at[left_slot], sibling).start()
 
             @pl.when(g + d < line)
             def _():
                 arrive(right_slot)
-                pl.when(has_left)(lambda: push(panel.at[right_slot], right_slot, send_line.at[right_slot], w - CORES).start())
+                pl.when(has_left & (d < far))(lambda: push(panel.at[right_slot], right_slot, send_line.at[right_slot], w - CORES).start())
                 push(panel.at[right_slot], right_slot, send_pair.at[right_slot], sibling).start()
+
+            @pl.when(helps & (d == far) & (h == 0))
+            def _():
+                pltpu.make_async_copy(guest, guest, recv_guest).wait()
+                high, low = halves(guest[...])
+                guest_high[...] = high
+                guest_low[...] = low
+
+            pl.when(helps & (d == far))(lambda: contract_guest(jnp.where(helps_left, right_slot, left_slot)))
 
             @pl.when(g - d >= 0)
             def _():
@@ -130,13 +169,35 @@
                 arrive(pair_right)
                 contract(panel[pair_right], pair_right)
 
-    @pl.loop(0, wide * PIECES)
-    def _(slot):
+            pl.when(helps & (d == far))(lambda: contract_guest(jnp.where(helps_left, pair_right, pair_left)))
+
+    def summed(slot):
         pltpu.make_async_copy(landed.at[slot], landed.at[slot], recv_sum.at[slot]).wait()
         total = part[slot, c]
         for k in range(cols - 1):
             total = total + landed[slot, k]
-        o_ref[:, pl.ds(pl.multiple_of(slot * rows, rows), rows)] = total
+        return total
+
+    def place(slot, block):
+        o_ref[:, pl.ds(pl.multiple_of(slot * rows, rows), rows)] = block
+
+    @pl.when(helps)
+    def _():
+        @pl.loop(0, extra)
+        def _(i):
+            outbox[i] = summed(slots + i)
+            give_back(i).start()
+
+    @pl.loop(0, slots)
+    def _(slot):
+        pl.when((slot >= first) & (slot < last))(lambda: place(slot, summed(slot)))
+
+    @pl.when(is_end)
+    def _():
+        @pl.loop(0, extra)
+        def _(i):
+            pltpu.make_async_copy(inbox.at[i], inbox.at[i], recv_back.at[i]).wait()
+            place(missing + i, inbox[i])
 
     for h in range(PIECES):
         slot = w * PIECES + h
@@ -144,7 +205,7 @@
         pl.when(has_left)(lambda: push(own(h), slot, send_line.at[wide * PIECES + h], w - CORES).wait_send())
         push(own(h), slot, send_pair.at[slot], sibling).wait_send()
 
-    @pl.loop(1, line)
+    @pl.loop(1, line - 1)
     def _(d):
         @pl.loop(0, PIECES)
         def _(h):
@@ -153,17 +214,29 @@
 
             @pl.when(g - d >= 0)
             def _():
-                pl.when(has_right)(lambda: push(panel.at[left_slot], left_slot, send_line.at[left_slot], w + CORES).wait_send())
+                pl.when(has_right & (d < far))(lambda: push(panel.at[left_slot], left_slot, send_line.at[left_slot], w + CORES).wait_send())
                 push(panel.at[left_slot], left_slot, send_pair.at[left_slot], sibling).wait_send()
 
             @pl.when(g + d < line)
             def _():
-                pl.when(has_left)(lambda: push(panel.at[right_slot], right_slot, send_line.at[right_slot], w - CORES).wait_send())
+                pl.when(has_left & (d < far))(lambda: push(panel.at[right_slot], right_slot, send_line.at[right_slot], w - CORES).wait_send())
                 push(panel.at[right_slot], right_slot, send_pair.at[right_slot], sibling).wait_send()
 
-    @pl.loop(0, wide * PIECES)
+    def sent(slot):
+        pltpu.make_async_copy(landed.at[slot], landed.at[slot], send_sum.at[slot]).wait()
+
+    @pl.loop(0, slots)
     def _(slot):
-        pltpu.make_async_copy(landed.at[slot], landed.at[slot], send_sum.at[slot]).wait()
+        pl.when((slot >= first) & (slot < last))(lambda: sent(slot))
+
+    @pl.when(helps)
+    def _():
+        @pl.loop(0, extra)
+        def _(i):
+            sent(slots + i)
+            give_back(i).wait_send()
+
+    pl.when(is_end)(lambda: lend().wait_send())
 
 
 def on_device(wide, cols, amplitudes, integrals):
@@ -171,6 +244,7 @@
     rows_b = integrals.shape[0]
     share = rows_a // cols
     slots = wide * PIECES
+    extra = CORES * PIECES
     rows = rows_b // PIECES
     vmem = pl.BlockSpec(memory_space=pltpu.VMEM)
     return pl.pallas_call(
@@ -182,13 +256,22 @@
             pltpu.VMEM((slots, rows, depth), jnp.float32),
             pltpu.VMEM((rows_a, depth), jnp.bfloat16),
             pltpu.VMEM((rows_a, depth), jnp.bfloat16),
-            pltpu.VMEM((slots, cols, share, rows), jnp.float32),
-            pltpu.VMEM((slots, cols - 1, share, rows), jnp.float32),
+            pltpu.VMEM((slots + extra, cols, share, rows), jnp.float32),
+            pltpu.VMEM((slots + extra, cols - 1, share, rows), jnp.float32),
+            pltpu.VMEM((rows_a, depth), jnp.float32),
+            pltpu.VMEM((rows_a, depth), jnp.bfloat16),
+            pltpu.VMEM((rows_a, depth), jnp.bfloat16),
+            pltpu.VMEM((extra, share, rows), jnp.float32),
+            pltpu.VMEM((extra, share, rows), jnp.float32),
             pltpu.SemaphoreType.DMA((slots + PIECES,)),
             pltpu.SemaphoreType.DMA((slots,)),
             pltpu.SemaphoreType.DMA((slots,)),
-            pltpu.SemaphoreType.DMA((slots,)),
-            pltpu.SemaphoreType.DMA((slots,)),
+            pltpu.SemaphoreType.DMA((slots + extra,)),
+            pltpu.SemaphoreType.DMA((slots + extra,)),
+            pltpu.SemaphoreType.DMA,
+            pltpu.SemaphoreType.DMA,
+            pltpu.SemaphoreType.DMA((extra,)),
+            pltpu.SemaphoreType.DMA((extra,)),
         ],
         compiler_params=pltpu.CompilerParams(
             collective_id=0, has_side_effects=True, vmem_limit_bytes=56 * 1024 * 1024),

time: 49.4 us -> 54.6 us (1.11)
  Pallas kernels: 47.3 us -> 52.5 us
    pallas_call x1, Pallas kernels: 47.3 us -> 52.5 us  [on_device(): pl.pallas_call(functools.partial(kernel, wide, cols), out_shape=jax.Shape...]
where the time goes in v3:
time: 54.6 us; the launch traced here: 54.4 us
  Pallas kernels  52.5 us (96%)
  local copies, waits for them, and re-layouts  1.87 us (3%)
    pallas_call x1, Pallas kernels, on_device(): pl.pallas_call(functools.partial(kernel, wide, cols), out_shape=jax.Shape...  52.5 us
    unnamed x1, local copies, waits for them, and re-layouts  1.87 us

profile of v3, /device:TPU:0, one launch (start us, length us, event | category | flops | bytes accessed | tf_op | source)
XLA Modules:
  0.0 54.4 jit_solution(6546860034570938387)
XLA Ops:
  0.0 52.5 %shard_map.28 = f32[64,2048]{1,0:T(8,128)} custom-call(f32[256,512]{1,0:T(8,128)} %a_ref.1, f32[256,512]{1,0:T(8,128)} %b_ref.1), custom_call_target="tpu_custom_call" | custom-call | tf_op jit(solution)/shard_map/pallas_call | solution.py:250
  52.5 1.9 %copy.4 = f32[64,2048]{1,0:T(8,128)} copy(f32[64,2048]{1,0:T(8,128)} %shard_map.28) | data formatting | bytes 1048576

commit v4 on v3

v4 whole, which is shorter than its diff:
```python
import functools

import jax
import jax.numpy as jnp
from jax import lax
from jax.experimental import pallas as pl
from jax.experimental.pallas import tpu as pltpu
from jax.sharding import PartitionSpec as P

MESH = pl.DeviceIdType.MESH
CORES = 2
PIECES = 2


def inner_factor(cols):
    return max(k for k in range(1, cols + 1) if cols % k == 0 and k * k <= cols)


def halves(x):
    high = x.astype(jnp.bfloat16)
    low = (x - high.astype(jnp.float32)).astype(jnp.bfloat16)
    return high, low


def dot(x, y):
    return lax.dot_general(x, y, (((1,), (1,)), ((), ())), preferred_element_type=jnp.float32)


def kernel(wide, cols, a_ref, b_ref, o_ref, panel, a_high, a_low, part, landed, mid, landed_mid,
           guest, guest_high, guest_low, outbox, inbox,
           send_line, send_pair, recv_panel, send_sum, recv_sum, send_mid, recv_mid,
           send_guest, recv_guest, send_back, recv_back):
    w = lax.axis_index("wide")
    c = lax.axis_index("col")
    line = wide // CORES
    g = w // CORES
    core = w % CORES
    sibling = g * CORES + 1 - core
    rows = b_ref.shape[0] // PIECES
    share = o_ref.shape[0]
    slots = wide * PIECES
    extra = CORES * PIECES
    far = line - 2
    left_end, right_end = g == 0, g == line - 1
    helps_left, helps_right = g == 1, g == far
    is_end = left_end | right_end
    helps = helps_left | helps_right
    partner = jnp.where(left_end | helps_right, w + CORES, w - CORES)
    first = jnp.where(right_end, extra, 0)
    last = jnp.where(left_end, slots - extra, slots)
    missing = jnp.where(left_end, slots - extra, 0)
    inner = inner_factor(cols)
    outer = cols // inner

    def route(h):
        if h % 2 == 0:
            return outer, inner, c // inner, c % inner, lambda f, s: f * inner + s
        return inner, outer, c % inner, c // inner, lambda f, s: s * inner + f

    barrier = pltpu.get_barrier_semaphore()

    def greet(wide_index, col_index):
        pl.semaphore_signal(barrier, inc=1, device_id={"wide": wide_index, "col": col_index}, device_id_type=MESH)

    has_left = g > 0
    has_right = g < line - 1
    pl.when(has_left)(lambda: greet(w - CORES, c))
    pl.when(has_right)(lambda: greet(w + CORES, c))
    greet(sibling, c)

    @pl.loop(1, cols)
    def _(j):
        greet(w, (c + j) % cols)

    pl.semaphore_wait(barrier, cols + has_left.astype(jnp.int32) + has_right.astype(jnp.int32))

    def push(src, slot, sem, target):
        return pltpu.make_async_remote_copy(
            src_ref=src, dst_ref=panel.at[slot], send_sem=sem, recv_sem=recv_panel.at[slot],
            device_id={"wide": target, "col": c}, device_id_type=MESH)

    def own(h):
        return b_ref.at[pl.ds(h * rows, rows)]

    def arrive(slot):
        pltpu.make_async_copy(panel.at[slot], panel.at[slot], recv_panel.at[slot]).wait()

    def lend():
        return pltpu.make_async_remote_copy(
            src_ref=a_ref, dst_ref=guest, send_sem=send_guest, recv_sem=recv_guest,
            device_id={"wide": partner, "col": c}, device_id_type=MESH)

    def give_back(i):
        return pltpu.make_async_remote_copy(
            src_ref=outbox.at[i], dst_ref=inbox.at[i], send_sem=send_back.at[i], recv_sem=recv_back.at[i],
            device_id={"wide": partner, "col": c}, device_id_type=MESH)

    def contract(block, slot, h):
        contract_rows(a_high, a_low, block, slot, h)

    def contract_guest(slot, h):
        contract_rows(guest_high, guest_low, panel[slot], slots + slot % extra, h)

    def contract_rows(rows_high, rows_low, block, slot, h):
        high, low = halves(block)
        product = dot(rows_high[...], high) + (dot(rows_high[...], low) + dot(rows_low[...], high))
        nf, ns, f, s, col_of = route(h)
        for i in range(nf):
            for k in range(ns):
                row = col_of(i, k) * share
                part[slot, i * ns + k] = product[row:row + share]

        for j in range(1, nf):
            peer = (f + j) % nf
            pltpu.make_async_remote_copy(
                src_ref=part.at[slot, pl.ds(peer * ns, ns)],
                dst_ref=landed.at[slot, pl.ds((nf - 1 - j) * ns, ns)],
                send_sem=send_sum.at[slot], recv_sem=recv_sum.at[slot],
                device_id={"wide": w, "col": col_of(peer, s)}, device_id_type=MESH).start()

    def take(ref, slot, count, sem):
        view = ref.at[slot, pl.ds(0, count)]
        pltpu.make_async_copy(view, view, sem.at[slot]).wait()

    def relay(slot, h):
        nf, ns, f, s, col_of = route(h)
        take(landed, slot, (nf - 1) * ns, recv_sum)
        total = part[slot, pl.ds(f * ns, ns)]
        for i in range(nf - 1):
            total = total + landed[slot, i * ns:(i + 1) * ns]
        mid[slot, 0:ns] = total
        for j in range(1, ns):
            peer = (s + j) % ns
            pltpu.make_async_remote_copy(
                src_ref=mid.at[slot, peer], dst_ref=landed_mid.at[slot, ns - 1 - j],
                send_sem=send_mid.at[slot], recv_sem=recv_mid.at[slot],
                device_id={"wide": w, "col": col_of(f, peer)}, device_id_type=MESH).start()

    for h in range(PIECES):
        slot = w * PIECES + h
        pl.when(has_right)(lambda: push(own(h), slot, send_line.at[slot], w + CORES).start())
        pl.when(has_left)(lambda: push(own(h), slot, send_line.at[wide * PIECES + h], w - CORES).start())
        push(own(h), slot, send_pair.at[slot], sibling).start()

    high, low = halves(a_ref[...])
    a_high[...] = high
    a_low[...] = low
    for h in range(PIECES):
        contract(b_ref[h * rows:(h + 1) * rows], w * PIECES + h, h)
    for h in range(PIECES):
        slot = sibling * PIECES + h
        arrive(slot)
        contract(panel[slot], slot, h)

    def relay_step(d, h):
        @pl.when(g - d >= 0)
        def _():
            relay((w - d * CORES) * PIECES + h, h)
            relay((sibling - d * CORES) * PIECES + h, h)

        @pl.when(g + d < line)
        def _():
            relay((w + d * CORES) * PIECES + h, h)
            relay((sibling + d * CORES) * PIECES + h, h)

    @pl.loop(1, line - 1)
    def _(d):
        for h in range(PIECES):
            left_slot = (w - d * CORES) * PIECES + h
            right_slot = (w + d * CORES) * PIECES + h
            pair_left = (sibling - d * CORES) * PIECES + h
            pair_right = (sibling + d * CORES) * PIECES + h

            @pl.when(g - d >= 0)
            def _():
                arrive(left_slot)
                pl.when(has_right & (d < far))(lambda: push(panel.at[left_slot], left_slot, send_line.at[left_slot], w + CORES).start())
                push(panel.at[left_slot], left_slot, send_pair.at[left_slot], sibling).start()

            @pl.when(g + d < line)
            def _():
                arrive(right_slot)
                pl.when(has_left & (d < far))(lambda: push(panel.at[right_slot], right_slot, send_line.at[right_slot], w - CORES).start())
                push(panel.at[right_slot], right_slot, send_pair.at[right_slot], sibling).start()

            pl.when(is_end & (d == (1 if h == PIECES - 1 else 0)))(lambda: lend().start())

            @pl.when(g - d >= 0)
            def _():
                contract(panel[left_slot], left_slot, h)

            @pl.when(g + d < line)
            def _():
                contract(panel[right_slot], right_slot, h)

            @pl.when(g - d >= 0)
            def _():
                arrive(pair_left)
                contract(panel[pair_left], pair_left, h)

            @pl.when(g + d < line)
            def _():
                arrive(pair_right)
                contract(panel[pair_right], pair_right, h)

            if h > 0:
                relay_step(d, h - 1)
            else:
                @pl.when(d == 1)
                def _():
                    for p in range(PIECES):
                        relay(w * PIECES + p, p)
                        relay(sibling * PIECES + p, p)

                pl.when(d > 1)(lambda: relay_step(d - 1, PIECES - 1))

    relay_step(line - 2, PIECES - 1)

    def summed(slot, h):
        nf, ns, f, s, col_of = route(h)
        take(landed_mid, slot, ns - 1, recv_mid)
        total = mid[slot, s]
        for k in range(ns - 1):
            total = total + landed_mid[slot, k]
        return total

    def place(slot, block):
        o_ref[:, pl.ds(pl.multiple_of(slot * rows, rows), rows)] = block

    @pl.when(helps)
    def _():
        pltpu.make_async_copy(guest, guest, recv_guest).wait()
        high, low = halves(guest[...])
        guest_high[...] = high
        guest_low[...] = low
        start = jnp.where(helps_left, slots - extra, 0)

        for i in range(extra):
            contract_guest(start + i, i % PIECES)
        for i in range(extra):
            relay(slots + i, i % PIECES)
        for i in range(extra):
            outbox[i] = summed(slots + i, i % PIECES)
            give_back(i).start()

    @pl.loop(0, wide)
    def _(q):
        for h in range(PIECES):
            slot = q * PIECES + h
            pl.when((slot >= first) & (slot < last))(lambda: place(slot, summed(slot, h)))

    @pl.when(is_end)
    def _():
        @pl.loop(0, extra)
        def _(i):
            pltpu.make_async_copy(inbox.at[i], inbox.at[i], recv_back.at[i]).wait()
            place(missing + i, inbox[i])

    for h in range(PIECES):
        slot = w * PIECES + h
        pl.when(has_right)(lambda: push(own(h), slot, send_line.at[slot], w + CORES).wait_send())
        pl.when(has_left)(lambda: push(own(h), slot, send_line.at[wide * PIECES + h], w - CORES).wait_send())
        push(own(h), slot, send_pair.at[slot], sibling).wait_send()

    @pl.loop(1, line - 1)
    def _(d):
        @pl.loop(0, PIECES)
        def _(h):
            left_slot = (w - d * CORES) * PIECES + h
            right_slot = (w + d * CORES) * PIECES + h

            @pl.when(g - d >= 0)
            def _():
                pl.when(has_right & (d < far))(lambda: push(panel.at[left_slot], left_slot, send_line.at[left_slot], w + CORES).wait_send())
                push(panel.at[left_slot], left_slot, send_pair.at[left_slot], sibling).wait_send()

            @pl.when(g + d < line)
            def _():
                pl.when(has_left & (d < far))(lambda: push(panel.at[right_slot], right_slot, send_line.at[right_slot], w - CORES).wait_send())
                push(panel.at[right_slot], right_slot, send_pair.at[right_slot], sibling).wait_send()

    def sent(slot, h):
        nf, ns, f, s, col_of = route(h)
        take(landed, slot, (nf - 1) * ns, send_sum)
        take(landed_mid, slot, ns - 1, send_mid)

    @pl.loop(0, wide)
    def _(q):
        for h in range(PIECES):
            slot = q * PIECES + h
            pl.when((slot >= first) & (slot < last))(lambda: sent(slot, h))

    @pl.when(helps)
    def _():
        for i in range(extra):
            sent(slots + i, i % PIECES)
            give_back(i).wait_send()

    pl.when(is_end)(lambda: lend().wait_send())


def on_device(wide, cols, amplitudes, integrals):
    rows_a, depth = amplitudes.shape
    rows_b = integrals.shape[0]
    share = rows_a // cols
    slots = wide * PIECES
    extra = CORES * PIECES
    rows = rows_b // PIECES
    vmem = pl.BlockSpec(memory_space=pltpu.VMEM)
    return pl.pallas_call(
        functools.partial(kernel, wide, cols),
        out_shape=jax.ShapeDtypeStruct((share, wide * rows_b), jnp.float32),
        in_specs=[vmem, vmem],
        out_specs=vmem,
        scratch_shapes=[
            pltpu.VMEM((slots, rows, depth), jnp.float32),
            pltpu.VMEM((rows_a, depth), jnp.bfloat16),
            pltpu.VMEM((rows_a, depth), jnp.bfloat16),
            pltpu.VMEM((slots + extra, cols, share, rows), jnp.float32),
            pltpu.VMEM((slots + extra, cols - 1, share, rows), jnp.float32),
            pltpu.VMEM((slots + extra, cols // inner_factor(cols), share, rows), jnp.float32),
            pltpu.VMEM((slots + extra, cols // inner_factor(cols) - 1, share, rows), jnp.float32),
            pltpu.VMEM((rows_a, depth), jnp.float32),
            pltpu.VMEM((rows_a, depth), jnp.bfloat16),
            pltpu.VMEM((rows_a, depth), jnp.bfloat16),
            pltpu.VMEM((extra, share, rows), jnp.float32),
            pltpu.VMEM((extra, share, rows), jnp.float32),
            pltpu.SemaphoreType.DMA((slots + PIECES,)),
            pltpu.SemaphoreType.DMA((slots,)),
            pltpu.SemaphoreType.DMA((slots,)),
            pltpu.SemaphoreType.DMA((slots + extra,)),
            pltpu.SemaphoreType.DMA((slots + extra,)),
            pltpu.SemaphoreType.DMA((slots + extra,)),
            pltpu.SemaphoreType.DMA((slots + extra,)),
            pltpu.SemaphoreType.DMA,
            pltpu.SemaphoreType.DMA,
            pltpu.SemaphoreType.DMA((extra,)),
            pltpu.SemaphoreType.DMA((extra,)),
        ],
        compiler_params=pltpu.CompilerParams(
            collective_id=0, has_side_effects=True, vmem_limit_bytes=56 * 1024 * 1024),
    )(amplitudes, integrals)


def solution(mesh):
    return jax.shard_map(
        functools.partial(on_device, mesh.shape["wide"], mesh.shape["col"]),
        mesh=mesh,
        in_specs=(P("wide", "col"), P("wide", "col")),
        out_specs=P(("wide", "col"), None),
        check_vma=False,
    )
```

time: 54.6 us -> 50.9 us (0.932)
  Pallas kernels: 52.5 us -> 48.8 us
    pallas_call x1, Pallas kernels: 52.5 us -> 48.8 us  [on_device(): pl.pallas_call(functools.partial(kernel, wide, cols), out_shape=jax.Shape...]
where the time goes in v4:
time: 50.9 us; the launch traced here: 50.7 us
  Pallas kernels  48.8 us (96%)
  local copies, waits for them, and re-layouts  1.87 us (4%)
    pallas_call x1, Pallas kernels, on_device(): pl.pallas_call(functools.partial(kernel, wide, cols), out_shape=jax.Shape...  48.8 us
    unnamed x1, local copies, waits for them, and re-layouts  1.87 us

profile of v4, /device:TPU:0, one launch (start us, length us, event | category | flops | bytes accessed | tf_op | source)
XLA Modules:
  0.0 50.7 jit_solution(17783134588955360037)
XLA Ops:
  0.0 48.8 %shard_map.28 = f32[64,2048]{1,0:T(8,128)} custom-call(f32[256,512]{1,0:T(8,128)} %a_ref.1, f32[256,512]{1,0:T(8,128)} %b_ref.1), custom_call_target="tpu_custom_call" | custom-call | tf_op jit(solution)/shard_map/pallas_call | solution.py:310
  48.8 1.9 %copy.4 = f32[64,2048]{1,0:T(8,128)} copy(f32[64,2048]{1,0:T(8,128)} %shard_map.28) | data formatting | bytes 1048576

commit v5 on v3

--- a/solution.py
+++ b/solution.py
@@ -10,6 +10,7 @@
 MESH = pl.DeviceIdType.MESH
 CORES = 2
 PIECES = 2
+LENT = PIECES - 1
 
 
 def halves(x):
@@ -35,16 +36,19 @@
     rows = b_ref.shape[0] // PIECES
     share = o_ref.shape[0]
     slots = wide * PIECES
-    extra = CORES * PIECES
+    extra = CORES
     far = line - 2
     left_end, right_end = g == 0, g == line - 1
     helps_left, helps_right = g == 1, g == far
     is_end = left_end | right_end
     helps = helps_left | helps_right
     partner = jnp.where(left_end | helps_right, w + CORES, w - CORES)
-    first = jnp.where(right_end, extra, 0)
-    last = jnp.where(left_end, slots - extra, slots)
-    missing = jnp.where(left_end, slots - extra, 0)
+    chip_slots = CORES * PIECES
+    missing = jnp.where(left_end, slots - chip_slots, 0) + LENT
+
+    def kept(slot):
+        lacks = (left_end & (slot >= slots - chip_slots)) | (right_end & (slot < chip_slots))
+        return ~(lacks & (slot % PIECES == LENT))
 
     barrier = pltpu.get_barrier_semaphore()
 
@@ -87,8 +91,8 @@
     def contract(block, slot):
         contract_rows(a_high, a_low, block, slot)
 
-    def contract_guest(slot):
-        contract_rows(guest_high, guest_low, panel[slot], slots + slot % extra)
+    def contract_guest(slot, i):
+        contract_rows(guest_high, guest_low, panel[slot], slots + i)
 
     def contract_rows(rows_high, rows_low, block, slot):
         high, low = halves(block)
@@ -120,7 +124,7 @@
         arrive(slot)
         contract(panel[slot], slot)
 
-    @pl.loop(1, line - 1)
+    @pl.loop(1, line)
     def _(d):
         @pl.loop(0, PIECES)
         def _(h):
@@ -128,48 +132,38 @@
             right_slot = (w + d * CORES) * PIECES + h
             pair_left = (sibling - d * CORES) * PIECES + h
             pair_right = (sibling + d * CORES) * PIECES + h
-            pl.when(is_end & (d == 2) & (h == 0))(lambda: lend().start())
-
-            @pl.when(g - d >= 0)
+
+            @pl.when((g - d >= 0) & ((d <= far) | (h < LENT)))
             def _():
                 arrive(left_slot)
-                pl.when(has_right & (d < far))(lambda: push(panel.at[left_slot], left_slot, send_line.at[left_slot], w + CORES).start())
+                pl.when(has_right & ((d < far) | ((d == far) & (h < LENT))))(lambda: push(panel.at[left_slot], left_slot, send_line.at[left_slot], w + CORES).start())
                 push(panel.at[left_slot], left_slot, send_pair.at[left_slot], sibling).start()
 
-            @pl.when(g + d < line)
+            @pl.when((g + d < line) & ((d <= far) | (h < LENT)))
             def _():
                 arrive(right_slot)
-                pl.when(has_left & (d < far))(lambda: push(panel.at[right_slot], right_slot, send_line.at[right_slot], w - CORES).start())
+                pl.when(has_left & ((d < far) | ((d == far) & (h < LENT))))(lambda: push(panel.at[right_slot], right_slot, send_line.at[right_slot], w - CORES).start())
                 push(panel.at[right_slot], right_slot, send_pair.at[right_slot], sibling).start()
 
-            @pl.when(helps & (d == far) & (h == 0))
-            def _():
-                pltpu.make_async_copy(guest, guest, recv_guest).wait()
-                high, low = halves(guest[...])
-                guest_high[...] = high
-                guest_low[...] = low
-
-            pl.when(helps & (d == far))(lambda: contract_guest(jnp.where(helps_left, right_slot, left_slot)))
-
-            @pl.when(g - d >= 0)
+            pl.when(is_end & (d == 1) & (h == PIECES - 1))(lambda: lend().start())
+
+            @pl.when((g - d >= 0) & ((d <= far) | (h < LENT)))
             def _():
                 contract(panel[left_slot], left_slot)
 
-            @pl.when(g + d < line)
+            @pl.when((g + d < line) & ((d <= far) | (h < LENT)))
             def _():
                 contract(panel[right_slot], right_slot)
 
-            @pl.when(g - d >= 0)
+            @pl.when((g - d >= 0) & ((d <= far) | (h < LENT)))
             def _():
                 arrive(pair_left)
                 contract(panel[pair_left], pair_left)
 
-            @pl.when(g + d < line)
+            @pl.when((g + d < line) & ((d <= far) | (h < LENT)))
             def _():
                 arrive(pair_right)
                 contract(panel[pair_right], pair_right)
-
-            pl.when(helps & (d == far))(lambda: contract_guest(jnp.where(helps_left, pair_right, pair_left)))
 
     def summed(slot):
         pltpu.make_async_copy(landed.at[slot], landed.at[slot], recv_sum.at[slot]).wait()
@@ -183,6 +177,16 @@
 
     @pl.when(helps)
     def _():
+        pltpu.make_async_copy(guest, guest, recv_guest).wait()
+        high, low = halves(guest[...])
+        guest_high[...] = high
+        guest_low[...] = low
+        start = jnp.where(helps_left, slots - chip_slots, 0) + LENT
+
+        @pl.loop(0, extra)
+        def _(i):
+            contract_guest(start + i * PIECES, i)
+
         @pl.loop(0, extra)
         def _(i):
             outbox[i] = summed(slots + i)
@@ -190,14 +194,14 @@
 
     @pl.loop(0, slots)
     def _(slot):
-        pl.when((slot >= first) & (slot < last))(lambda: place(slot, summed(slot)))
+        pl.when(kept(slot))(lambda: place(slot, summed(slot)))
 
     @pl.when(is_end)
     def _():
         @pl.loop(0, extra)
         def _(i):
             pltpu.make_async_copy(inbox.at[i], inbox.at[i], recv_back.at[i]).wait()
-            place(missing + i, inbox[i])
+            place(missing + i * PIECES, inbox[i])
 
     for h in range(PIECES):
         slot = w * PIECES + h
@@ -205,21 +209,21 @@
         pl.when(has_left)(lambda: push(own(h), slot, send_line.at[wide * PIECES + h], w - CORES).wait_send())
         push(own(h), slot, send_pair.at[slot], sibling).wait_send()
 
-    @pl.loop(1, line - 1)
+    @pl.loop(1, line)
     def _(d):
         @pl.loop(0, PIECES)
         def _(h):
             left_slot = (w - d * CORES) * PIECES + h
             right_slot = (w + d * CORES) * PIECES + h
 
-            @pl.when(g - d >= 0)
-            def _():
-                pl.when(has_right & (d < far))(lambda: push(panel.at[left_slot], left_slot, send_line.at[left_slot], w + CORES).wait_send())
+            @pl.when((g - d >= 0) & ((d <= far) | (h < LENT)))
+            def _():
+                pl.when(has_right & ((d < far) | ((d == far) & (h < LENT))))(lambda: push(panel.at[left_slot], left_slot, send_line.at[left_slot], w + CORES).wait_send())
                 push(panel.at[left_slot], left_slot, send_pair.at[left_slot], sibling).wait_send()
 
-            @pl.when(g + d < line)
-            def _():
-                pl.when(has_left & (d < far))(lambda: push(panel.at[right_slot], right_slot, send_line.at[right_slot], w - CORES).wait_send())
+            @pl.when((g + d < line) & ((d <= far) | (h < LENT)))
+            def _():
+                pl.when(has_left & ((d < far) | ((d == far) & (h < LENT))))(lambda: push(panel.at[right_slot], right_slot, send_line.at[right_slot], w - CORES).wait_send())
                 push(panel.at[right_slot], right_slot, send_pair.at[right_slot], sibling).wait_send()
 
     def sent(slot):
@@ -227,7 +231,7 @@
 
     @pl.loop(0, slots)
     def _(slot):
-        pl.when((slot >= first) & (slot < last))(lambda: sent(slot))
+        pl.when(kept(slot))(lambda: sent(slot))
 
     @pl.when(helps)
     def _():
@@ -244,7 +248,7 @@
     rows_b = integrals.shape[0]
     share = rows_a // cols
     slots = wide * PIECES
-    extra = CORES * PIECES
+    extra = CORES
     rows = rows_b // PIECES
     vmem = pl.BlockSpec(memory_space=pltpu.VMEM)
     return pl.pallas_call(

time: 54.6 us -> 44.6 us (0.82)
  Pallas kernels: 52.5 us -> 42.5 us
    pallas_call x1, Pallas kernels: 52.5 us -> 42.5 us  [on_device(): pl.pallas_call(functools.partial(kernel, wide, cols), out_shape=jax.Shape...]
where the time goes in v5:
time: 44.6 us; the launch traced here: 44.4 us
  Pallas kernels  42.5 us (95%)
  local copies, waits for them, and re-layouts  1.87 us (4%)
    pallas_call x1, Pallas kernels, on_device(): pl.pallas_call(functools.partial(kernel, wide, cols), out_shape=jax.Shape...  42.5 us
    unnamed x1, local copies, waits for them, and re-layouts  1.87 us

profile of v5, /device:TPU:0, one launch (start us, length us, event | category | flops | bytes accessed | tf_op | source)
XLA Modules:
  0.0 44.4 jit_solution(8297918500405212770)
XLA Ops:
  0.0 42.5 %shard_map.28 = f32[64,2048]{1,0:T(8,128)} custom-call(f32[256,512]{1,0:T(8,128)} %a_ref.1, f32[256,512]{1,0:T(8,128)} %b_ref.1), custom_call_target="tpu_custom_call" | custom-call | tf_op jit(solution)/shard_map/pallas_call | solution.py:254
  42.5 1.9 %copy.4 = f32[64,2048]{1,0:T(8,128)} copy(f32[64,2048]{1,0:T(8,128)} %shard_map.28) | data formatting | bytes 1048576

commit v6 on v5

--- a/solution.py
+++ b/solution.py
@@ -23,7 +23,7 @@
     return lax.dot_general(x, y, (((1,), (1,)), ((), ())), preferred_element_type=jnp.float32)
 
 
-def kernel(wide, cols, a_ref, b_ref, o_ref, panel, a_high, a_low, part, landed,
+def kernel(wide, cols, a_hbm, b_hbm, o_ref, a_ref, b_ref, load_sem, panel, a_high, a_low, part, landed,
            guest, guest_high, guest_low, outbox, inbox,
            send_line, send_pair, recv_panel, send_sum, recv_sum,
            send_guest, recv_guest, send_back, recv_back):
@@ -50,6 +50,10 @@
         lacks = (left_end & (slot >= slots - chip_slots)) | (right_end & (slot < chip_slots))
         return ~(lacks & (slot % PIECES == LENT))
 
+    load_a = pltpu.make_async_copy(a_hbm, a_ref, load_sem.at[0])
+    load_b = pltpu.make_async_copy(b_hbm, b_ref, load_sem.at[1])
+    load_b.start()
+    load_a.start()
     barrier = pltpu.get_barrier_semaphore()
 
     def greet(wide_index, col_index):
@@ -66,6 +70,8 @@
         greet(w, (c + j) % cols)
 
     pl.semaphore_wait(barrier, cols + has_left.astype(jnp.int32) + has_right.astype(jnp.int32))
+
+    load_b.wait()
 
     def push(src, slot, sem, target):
         return pltpu.make_async_remote_copy(
@@ -114,6 +120,7 @@
         pl.when(has_left)(lambda: push(own(h), slot, send_line.at[wide * PIECES + h], w - CORES).start())
         push(own(h), slot, send_pair.at[slot], sibling).start()
 
+    load_a.wait()
     high, low = halves(a_ref[...])
     a_high[...] = high
     a_low[...] = low
@@ -254,9 +261,12 @@
     return pl.pallas_call(
         functools.partial(kernel, wide, cols),
         out_shape=jax.ShapeDtypeStruct((share, wide * rows_b), jnp.float32),
-        in_specs=[vmem, vmem],
+        in_specs=[pl.BlockSpec(memory_space=pl.ANY)] * 2,
         out_specs=vmem,
         scratch_shapes=[
+            pltpu.VMEM((rows_a, depth), jnp.float32),
+            pltpu.VMEM((rows_b, depth), jnp.float32),
+            pltpu.SemaphoreType.DMA((2,)),
             pltpu.VMEM((slots, rows, depth), jnp.float32),
             pltpu.VMEM((rows_a, depth), jnp.bfloat16),
             pltpu.VMEM((rows_a, depth), jnp.bfloat16),

time: 44.6 us -> 43.4 us (0.973)
  Pallas kernels: 42.5 us -> 41.3 us
    pallas_call x1, Pallas kernels: 42.5 us -> 41.3 us  [on_device(): pl.pallas_call(functools.partial(kernel, wide, cols), out_shape=jax.Shape...]
where the time goes in v6:
time: 43.4 us; the launch traced here: 43.2 us
  Pallas kernels  41.3 us (95%)
  local copies, waits for them, and re-layouts  1.87 us (4%)
    pallas_call x1, Pallas kernels, on_device(): pl.pallas_call(functools.partial(kernel, wide, cols), out_shape=jax.Shape...  41.3 us
    unnamed x1, local copies, waits for them, and re-layouts  1.87 us

profile of v6, /device:TPU:0, one launch (start us, length us, event | category | flops | bytes accessed | tf_op | source)
XLA Modules:
  0.0 43.2 jit_solution(7579419902360203111)
XLA Ops:
  0.0 41.3 %shard_map.28 = f32[64,2048]{1,0:T(8,128)} custom-call(f32[256,512]{1,0:T(8,128)} %a_hbm.1, f32[256,512]{1,0:T(8,128)} %b_hbm.1), custom_call_target="tpu_custom_call" | custom-call | tf_op jit(solution)/shard_map/pallas_call | solution.py:261
  41.4 1.9 %copy.4 = f32[64,2048]{1,0:T(8,128)} copy(f32[64,2048]{1,0:T(8,128)} %shard_map.28) | data formatting | bytes 1048576
